TPU v7x, 32 devices: a whole 2x2x4 slice. The times are simulated.
32 devices in a mesh: ctx: 8 (over z, x), tp: 4 (over y, core).
Axes of the slice: x: 2, y: 2, z: 4, core: 2. Of those that a mesh axis runs over, the one named last changes fastest.
Arguments:
- tokens: bfloat16 [4096, 4096], P(('ctx', 'tp')), may hold values from -6 to 6
- in_weight: bfloat16 [4096, 3, 4096], P('ctx', None, 'tp'), may hold values from -0.09375 to 0.09375
- short_filter: float32 [3, 3, 4096], P(None, None, 'tp'), may hold values from -3 to 3
- decay_rates: float32 [16, 4096], P(None, 'tp'), may hold values from 1.2207031e-05 to 0.1, as said below
- residues: float32 [16, 4096], P(None, 'tp'), may hold values from -1.5 to 1.5
- skip_gain: float32 [4096], P('tp'), may hold values from -4 to 4
Outputs:
- mixed: bfloat16 [4096, 4096], P('ctx', 'tp')
Inputs may be any that keep to these rules, and one draw needn't show every extreme that they name: `decay_rates`: positive decay rates.
All inputs are finite; a program needn't handle non-finite values.
Results may differ from a plain program's by a relative error of at most 0.0063.
Values may be sent and summed in bfloat16 or wider, within the bound.
A program may use at most 128 MiB of HBM per device.

v0:
```python
import jax
import jax.numpy as jnp
from jax import lax
from jax.sharding import PartitionSpec as P

BLOCK = 32


def passed_along(value, axis, steps):
    count = lax.axis_size(axis)
    initial, last = (max(0, -steps), min(count, count - steps))
    return lax.ppermute(value, axis, [(source, source + steps) for source in range(initial, last)])


def block_scan(product, decay_rates, residues, block):
    channels = product.shape[1]
    mode_gain = residues * jnp.sqrt(2.0 * decay_rates)
    positions = jnp.arange(block, dtype=jnp.float32)
    kernel = jnp.sum(
        mode_gain[None] * jnp.exp(-decay_rates[None] * positions[:, None, None]), axis=1
    )
    gaps = jnp.arange(block, dtype=jnp.int32)[:, None] - jnp.arange(block, dtype=jnp.int32)[None, :]
    toeplitz = jnp.where(
        (gaps >= 0)[:, :, None], kernel[jnp.clip(gaps, 0, block - 1)], jnp.float32(0.0)
    )
    read_out = mode_gain[None] * jnp.exp(-decay_rates[None] * (positions[:, None, None] + 1.0))
    take_in = jnp.exp(-decay_rates[None] * (block - 1.0 - positions)[:, None, None])
    step_decay = jnp.exp(-decay_rates * block)

    def advance(state, block_in):
        block_out = jnp.sum(toeplitz * block_in[None], axis=1) + jnp.sum(
            read_out * state[None], axis=1
        )
        state = step_decay * state + jnp.sum(take_in * block_in[:, None, :], axis=0)
        return (state, block_out)

    zero_state = jnp.zeros(decay_rates.shape, jnp.float32)
    state, outputs = lax.scan(advance, zero_state, product.reshape(-1, block, channels))
    return (outputs.reshape(-1, channels), state)


def per_device(tokens, in_weight, short_filter, decay_rates, residues, skip_gain):
    gathered = lax.all_gather(tokens, "tp", axis=0, tiled=True)
    length = gathered.shape[0]
    channels = in_weight.shape[2]
    short_lag = short_filter.shape[1] - 1
    flat_weight = in_weight.reshape(in_weight.shape[0], 3 * channels)
    projected = jnp.dot(
        gathered,
        lax.all_gather(flat_weight, "ctx", axis=0, tiled=True),
        preferred_element_type=jnp.float32,
    ).astype(jnp.bfloat16)
    prior_rows = passed_along(projected[length - short_lag :], "ctx", 1)
    padded = jnp.concatenate([prior_rows, projected], axis=0)
    widened = padded.astype(jnp.float32).reshape(length + short_lag, 3, channels)
    features = jnp.zeros((length, 3, channels), jnp.float32)
    for offset in range(short_lag + 1):
        features = (
            features
            + short_filter[None, :, offset, :]
            * widened[short_lag - offset : short_lag - offset + length]
        )
    product = features[:, 1] * features[:, 2]
    inside, outgoing = block_scan(product, decay_rates, residues, BLOCK)
    every_state = lax.all_gather(outgoing[None], "ctx", axis=0, tiled=True)
    shard_count = every_state.shape[0]
    own_index = lax.axis_index("ctx")
    sources = jnp.arange(shard_count, dtype=jnp.int32)
    distance = own_index - 1 - sources
    earlier = distance >= 0
    steps_back = jnp.where(earlier, distance, 0).astype(jnp.float32)
    factors = jnp.exp(-decay_rates[None] * (length * steps_back)[:, None, None])
    factors = jnp.where(earlier[:, None, None], factors, jnp.float32(0.0))
    incoming = jnp.sum(factors * every_state, axis=0)
    mode_gain = residues * jnp.sqrt(2.0 * decay_rates)
    offsets = jnp.arange(1, length + 1, dtype=jnp.float32)
    carried = jnp.sum(
        mode_gain[None] * jnp.exp(-decay_rates[None] * offsets[:, None, None]) * incoming[None],
        axis=1,
    )
    longconv = inside + carried
    return (features[:, 0] * (longconv + skip_gain[None] * product)).astype(jnp.bfloat16)


def solution(mesh):
    in_specs = (
        P(("ctx", "tp"), None),
        P("ctx", None, "tp"),
        P(None, None, "tp"),
        P(None, "tp"),
        P(None, "tp"),
        P("tp"),
    )
    out_specs = P("ctx", "tp")
    return jax.shard_map(
        per_device, mesh=mesh, in_specs=in_specs, out_specs=out_specs, check_vma=False
    )
```

profile of v0, /device:TPU:0, one launch (start us, length us, event | category | flops | bytes accessed | tf_op | source)
XLA Modules:
  0.0 757.3 jit_solution(17259507543595357559)
XLA Ops:
  7.3 4.6 copy.24
  12.7 5.4 gather_fusion
  18.2 4.9 broadcast_select_fusion.1
  23.2 22.9 %all-gather.4.cloned.1.call-done = bf16[512,4096]{1,0:T(8,128)(2,1)} async-done(((bf16[128,4096]{1,0:T(8,128)(2,1)}), bf16[512,4096]{1,0:T(8,128)(2,1)}) %all-gather.4.cloned.1.call-update) | async-done | bytes 4194320 | tf_op jit(solution)/shard_map/all_gather | solution.py:43
  46.1 481.9 %all-gather.6.cloned.1.call-done = bf16[4096,3072]{0,1:T(8,128)(2,1)} async-done(((bf16[512,3072]{0,1:T(8,128)(2,1)}), bf16[4096,3072]{0,1:T(8,128)(2,1)}) %all-gather.6.cloned.1.call-update) | async-done | bytes 25165840 | tf_op jit(solution)/shard_map/all_gather | solution.py:50
  528.0 18.2 %convolution_convert_fusion = bf16[512,3072]{1,0:T(8,128)(2,1)S(1)} fusion(bf16[512,4096]{1,0:T(8,128)(2,1)} %all-gather.4.cloned.1.call-done, bf16[4096,3072]{0,1:T(8,128)(2,1)} %all-gather.6.cloned.1.call-done), kind=kOutput, calls=%fused_computation.14 | convolution fusion | flops 12886474752 | bytes 32505856 | tf_op jit(solution)/shard_map/dot_general | solution.py:48
  552.8 6.6 fusion.10
  559.4 6.6 copy.29
  566.0 6.6 copy.30
  572.5 6.6 copy.27
  579.1 6.6 copy.28
  585.7 6.6 copy.25
  592.3 6.5 copy.26
  598.8 8.8 %multiply_add_fusion.1 = f32[512,3,1024]{2,0,1:T(8,128)S(1)} fusion(f32[512,3,1024]{2,0,1:T(8,128)} %copy.30, f32[512,3,1024]{2,0,1:T(8,128)} %copy.28, f32[512,3,1024]{2,0,1:T(8,128)} %copy.26, f32[3,1024]{1,0:T(4,128)S(1)} %get-tuple-element.187, f32[3,1024]{1,0:T(4,128)S(1)} %get-tuple-element.188, f32[3,1024]{1,0:T(4,128)S(1)} %bitcast.51), kind=kLoop, calls=%fused_computation.13 | loop fusion | flops 7864320 | bytes 25202688 | tf_op jit(solution)/shard_map/add | solution.py:59
  612.0 90.5 %while.15 = (s32[]{:T(128)}, f32[16,1024]{1,0:T(8,128)S(1)}, f32[16,32,1024]{2,1,0:T(8,128)}, f32[16,1024]{1,0:T(8,128)S(1)}, f32[16,32,1024]{2,1,0:T(8,128)}, /...) while((s32[]{:T(128)}, f32[16,1024]{1,0:T(8,128)S(1)}, ...), condition=%wide.region_5.6_spmd.clone.clone.clone, body=%wide.region_1.5_spmd.clone.clone.clone.sunk | while | flops 5783555 | bytes 6029712 | solution.py:38
  614.1 2.9 multiply_reduce_fusion.5
  619.8 2.9 multiply_reduce_fusion.5
  625.4 2.9 multiply_reduce_fusion.5
  631.1 2.9 multiply_reduce_fusion.5
  636.7 2.9 multiply_reduce_fusion.5
  642.4 2.9 multiply_reduce_fusion.5
  648.1 2.9 multiply_reduce_fusion.5
  702.6 34.3 %all-gather = f32[128,1024]{1,0:T(8,128)S(1)} all-gather(f32[16,1024]{1,0:T(8,128)S(1)} %get-tuple-element.49), channel_id=2, replica_groups=mesh['ctx'=8,'tp'=4] {'ctx'}, dimensions={0}, use_global_device_ids=true | all-gather | bytes 589824 | tf_op jit(solution)/shard_map/all_gather | solution.py:65
  737.1 11.0 %multiply_reduce_fusion.1 = f32[512,1024]{1,0:T(8,128)S(1)} fusion(f32[16,1024]{1,0:T(8,128)S(1)} %multiply_reduce_fusion.3, f32[512]{0:T(512)S(1)} %iota_add_fusion, f32[16,1024]{1,0:T(8,128)S(1)} %get-tuple-element.298, f32[16,1024]{1,0:T(8,128)S(1)} %get-tuple-element.299), kind=kLoop, calls=%fused_computation.12 | loop fusion | flops 33030144 | bytes 2295808 | tf_op jit(solution)/shard_map/reduce_sum | solution.py:77
  (134 shorter events, 84.8 us)
Async XLA Ops:
  6.5 39.6 %all-gather.4.cloned.1.call-start = ((), (), s32[]{:S(2)}) async-start(), calls=%async_computation | async-start | bytes 5242880 | tf_op jit(solution)/shard_map/all_gather | solution.py:43
  7.3 4.8 copy-start.3
  7.3 4.8 copy-start.4
  7.3 520.8 %all-gather.6.cloned.1.call-start = ((), (), s32[]{:S(2)}) async-start(), calls=%async_computation.1 | async-start | bytes 28311552 | tf_op jit(solution)/shard_map/all_gather | solution.py:50
  12.7 5.5 copy-start.5
  546.2 2.5 copy-start.1
  546.3 3.7 collective-permute-start
  607.6 2.7 copy-start
  736.9 11.3 %slice-start = ((s8[6291456]{0:T(1024)(128)(4,1)}), s8[4194304]{0:T(1024)(128)(4,1)S(1)}, s32[]{:S(2)}) async-start(s8[6291456]{0:T(1024)(128)(4,1)} %bitcast.42), calls=%async_computation.2 | async-start | bytes 8388608
  737.1 11.1 %slice-start.1 = ((s8[6291456]{0:T(1024)(128)(4,1)}), s8[2097152]{0:T(1024)(128)(4,1)S(1)}, s32[]{:S(2)}) async-start(s8[6291456]{0:T(1024)(128)(4,1)} %bitcast.42), calls=%async_computation.3 | async-start | bytes 4194304
  737.1 11.1 %copy-start.2 = (f32[16,32,1024]{2,1,0:T(8,128)S(1)}, f32[16,32,1024]{2,1,0:T(8,128)}, u32[]{:S(2)}) copy-start(f32[16,32,1024]{2,1,0:T(8,128)} %get-tuple-element.48) | copy-start | bytes 6291460
  737.1 11.1 %copy-start.6 = (f32[1024]{0:T(1024)S(1)}, f32[1024]{0:T(1024)}, u32[]{:S(2)}) copy-start(f32[1024]{0:T(1024)} %param.13) | copy-start | bytes 12292
Sparse Core Ops, SparseCore 0:
  8.9 37.1 all-gather.3
  47.6 480.3 all-gather.5
where the time goes:
time: 759 us; the launch traced here: 757 us
  waiting for transfers between devices  507 us (67%)
  other arithmetic  108 us (14%)
  local copies, waits for them, and re-layouts  73.6 us (10%)
  blocking collectives  34.3 us (5%)
  matrix products  18.2 us (2%)
  between operations  13.7 us (2%)
    all_gather x1, waiting for transfers between devices, per_device(): lax.all_gather(flat_weight, 'ctx', axis=0, tiled=True)  482 us
    reduce_sum x16, other arithmetic, advance(): jnp.sum(toeplitz * block_in[None], axis=1)  46.5 us
    slice x7, local copies, waits for them, and re-layouts, per_device(): widened[short_lag - offset:short_lag - offset + length]  46 us
    all_gather x1, blocking collectives, per_device(): every_state = lax.all_gather(outgoing[None], 'ctx', axis=0, tiled=True)  34.3 us
    all_gather x1, waiting for transfers between devices, per_device(): gathered = lax.all_gather(tokens, 'tp', axis=0, tiled=True)  22.9 us
    dot_general x1, matrix products, per_device(): jnp.dot(gathered, lax.all_gather(flat_weight, 'ctx', axis=0, tiled=True),...  18.2 us
    reduce_sum x16, other arithmetic, advance(): jnp.sum(read_out * state[None], axis=1)  17.7 us
  transfers between devices with their start and end apart: 3, of which 3 were waited for; matrix products, arithmetic and copies ran while one was open for 2% of the time, Pallas kernels for 0%

commit v1 on v0

v1 whole, which is shorter than its diff:
```python
import functools

import jax
import jax.numpy as jnp
from jax import lax
from jax.experimental import pallas as pl
from jax.experimental.pallas import tpu as pltpu
from jax.sharding import PartitionSpec as P

MESH = pl.DeviceIdType.MESH
VMEM_BYTES = 60 * 1024 * 1024
SUBLANES = 8
TAIL = 16
LANES = 128


def flipped(index, bit):
    return index + bit - 2 * bit * ((index // bit) % 2)


def gather_kernel(Z, X, T, tok_ref, w_ref, out_ref, tok, w, tok_recv, w_recv, send_z, send_t, send_wz, send_wx, own_sem):
    ctx, t = lax.axis_index("ctx"), lax.axis_index("tp")
    z, x = ctx // X, ctx % X
    bits = []
    bit = T // 2
    while bit:
        bits.append(bit)
        bit //= 2

    own_tok = pltpu.make_async_copy(tok_ref, tok.at[z, t], own_sem.at[0])
    own_w = pltpu.make_async_copy(w_ref.at[z], w.at[z, x], own_sem.at[1])
    own_tok.start()
    own_w.start()

    barrier = pltpu.get_barrier_semaphore()
    for o in range(1, Z):
        pl.semaphore_signal(barrier, inc=1, device_id=(((z + o) % Z) * X + x, t), device_id_type=MESH)
    for o in range(1, X):
        pl.semaphore_signal(barrier, inc=1, device_id=(z * X + (x + o) % X, t), device_id_type=MESH)
    for bit in bits:
        pl.semaphore_signal(barrier, inc=1, device_id=(ctx, flipped(t, bit)), device_id_type=MESH)
    pl.semaphore_wait(barrier, Z - 1 + X - 1 + len(bits))

    def remote(src, dst, send, recv, device):
        return pltpu.make_async_remote_copy(
            src_ref=src, dst_ref=dst, send_sem=send, recv_sem=recv, device_id=device, device_id_type=MESH
        )

    def tok_line(side, source, src):
        to = z + 1 if side == 0 else z - 1
        return remote(
            src, tok.at[source, t], send_z.at[side, source], tok_recv.at[source, t], (to * X + x, t)
        )

    def exists(side, s):
        return z - s >= 0 if side == 0 else z + s < Z

    def held(level):
        masks = [0]
        for bit in bits[:level]:
            masks = masks + [m + bit for m in masks]
        return masks

    def slot(mask):
        index = t
        for bit in bits:
            if mask & bit:
                index = flipped(index, bit)
        return index

    def tp_copies(level, source, own):
        copies = []
        for mask in held(level):
            q = slot(mask)
            src = tok_ref if own and mask == 0 else tok.at[source, q]
            copies.append(
                remote(
                    src,
                    tok.at[source, q],
                    send_t.at[level, source, mask],
                    tok_recv.at[source, q],
                    (ctx, flipped(t, bits[level])),
                )
            )
        return copies

    def tok_arrived(source, q):
        remote(tok.at[source, q], tok.at[source, q], own_sem.at[0], tok_recv.at[source, q], (ctx, t)).wait_recv()

    def w_line(target):
        return remote(w_ref.at[target], w.at[z, x], send_wz.at[target], w_recv.at[z, x], (target * X + x, t))

    def w_cross(source, o, src):
        return remote(
            src, w.at[source, x], send_wx.at[source, o], w_recv.at[source, x], (z * X + (x + o) % X, t)
        )

    def w_arrived(source, q):
        remote(w.at[source, q], w.at[source, q], own_sem.at[0], w_recv.at[source, q], (ctx, t)).wait_recv()

    def multiply(source):
        depth = w.shape[0] * w.shape[1] * w.shape[2]
        rows = tok.shape[1] * tok.shape[2]
        a = tok.at[source].reshape(rows, depth)
        b = w.reshape(depth, w.shape[3])
        tile = 256 if w.shape[3] % 256 == 0 else 128

        @pl.loop(0, w.shape[3] // tile)
        def _(n):
            cols = pl.ds(pl.multiple_of(n * tile, tile), tile)
            out_ref[source, :, cols] = jnp.dot(
                a[...], b[:, cols], preferred_element_type=jnp.float32
            ).astype(out_ref.dtype)

    for side in (0, 1):
        @pl.when(z + 1 < Z if side == 0 else z >= 1)
        def _():
            tok_line(side, z, tok_ref).start()
    for o in range(1, X):
        w_cross(z, o, w_ref.at[z]).start()
    for s in range(Z - 1, 0, -1):
        for side in (0, 1):
            @pl.when(z + s < Z if side == 0 else z >= s)
            def _():
                w_line(z + s if side == 0 else z - s).start()

    def start_level(level, s):
        for side in (0, 1):
            if s == 0 and side == 1:
                continue

            def act():
                source = z - s if side == 0 else z + s
                if level > 0:
                    for mask in held(level - 1):
                        tok_arrived(source, slot(mask + bits[level - 1]))
                for copy in tp_copies(level, source, s == 0):
                    copy.start()

            if s == 0:
                act()
            else:
                pl.when(exists(side, s))(act)

    def take_line(s):
        for side in (0, 1):
            @pl.when(exists(side, s))
            def _():
                source = z - s if side == 0 else z + s
                tok_arrived(source, t)

                @pl.when(z + 1 < Z if side == 0 else z >= 1)
                def _():
                    tok_line(side, source, tok.at[source, t]).start()

    def finish(s):
        for side in (0, 1):
            if s == 0 and side == 1:
                continue

            def act():
                source = z - s if side == 0 else z + s
                for mask in held(len(bits) - 1):
                    tok_arrived(source, slot(mask + bits[-1]))
                multiply(source)

            if s == 0:
                act()
            else:
                pl.when(exists(side, s))(act)

    def take_w(s):
        for side in (0, 1):
            @pl.when(exists(side, s))
            def _():
                source = z - s if side == 0 else z + s
                w_arrived(source, x)
                for o in range(1, X):
                    w_cross(source, o, w.at[source, x]).start()

    start_level(0, 0)
    take_line(1)
    start_level(0, 1)
    for level in range(1, len(bits)):
        start_level(level, 0)
        start_level(level, 1)
    for s in range(Z - 1, 0, -1):
        take_w(s)
    own_tok.wait()
    own_w.wait()
    if Z > 2:
        take_line(2)
        start_level(0, 2)
    for source in range(Z):
        for o in range(1, X):
            w_arrived(source, (x + o) % X)
    finish(0)
    finish(1)
    for s in range(2, Z):
        if s > 2:
            take_line(s)
            start_level(0, s)
        for level in range(1, len(bits)):
            start_level(level, s)
        finish(s)

    for side in (0, 1):
        for s in range(Z - 1):
            @pl.when(jnp.logical_and(exists(side, s), z + 1 < Z if side == 0 else z >= 1))
            def _():
                source = z - s if side == 0 else z + s
                tok_line(side, source, tok.at[source, t]).wait_send()
    for source in range(Z):
        for o in range(1, X):
            w_cross(source, o, w.at[source, x]).wait_send()
        for level in range(len(bits)):
            for copy in tp_copies(level, source, False):
                copy.wait_send()
    for o in range(1, Z):
        w_line((z + o) % Z).wait_send()


def conv_kernel(Z, X, proj_ref, filt_ref, dec_ref, res_ref, skip_ref, out_ref,
                halo, wid, prod, gate, consts, st, seg, allseg, outbuf,
                halo_sems, seg_send, seg_recv, out_send, out_recv, own_sem):
    ctx, t = lax.axis_index("ctx"), lax.axis_index("tp")
    z, x = ctx // X, ctx % X
    groups, L = prod.shape[1], prod.shape[2]
    C = groups * LANES
    modes = dec_ref.shape[0]
    lags = filt_ref.shape[0] // 3
    steps = L // SUBLANES
    lane0 = pl.multiple_of(z * C, LANES)
    cols = pl.ds(lane0, C)

    barrier = pltpu.get_barrier_semaphore()
    for o in range(1, Z):
        pl.semaphore_signal(barrier, inc=1, device_id=(((z + o) % Z) * X + x, t), device_id_type=MESH)
    for o in range(1, X):
        pl.semaphore_signal(barrier, inc=1, device_id=(z * X + (x + o) % X, t), device_id_type=MESH)
    pl.semaphore_wait(barrier, Z - 1 + X - 1)

    tails = pltpu.make_async_remote_copy(
        src_ref=proj_ref.at[:, pl.ds(L - TAIL, TAIL), :], dst_ref=halo,
        send_sem=halo_sems.at[0], recv_sem=halo_sems.at[1],
        device_id=(z * X + (x + 1) % X, t), device_id_type=MESH,
    )
    tails.start()

    dec = dec_ref[:, cols]
    gain = res_ref[:, cols] * jnp.sqrt(2.0 * dec)
    decay = jnp.exp(-dec)
    sub_decay = jnp.exp(-dec * steps)
    seg_decay = jnp.exp(-dec * L)
    for m in range(modes):
        consts[0, m] = jnp.broadcast_to(decay[m : m + 1], (SUBLANES, C))
        consts[1, m] = jnp.broadcast_to(gain[m : m + 1], (SUBLANES, C))
    skip = skip_ref[:, cols]
    filt = filt_ref[:, cols]
    tails.wait()

    rows = 32

    @pl.loop(0, Z)
    def _(s):
        before = jnp.where(x == 0, s - 1, s)
        tail = halo[jnp.maximum(before, 0)].astype(jnp.float32)
        wid[0:SUBLANES] = jnp.where(before >= 0, tail[TAIL - SUBLANES :], 0.0)
        wid[SUBLANES:] = proj_ref[s].astype(jnp.float32)

        @pl.loop(0, L // rows)
        def _(r):
            start = pl.multiple_of(r * rows, rows)
            feats = []
            for j in range(3):
                block = wid[pl.ds(start, rows + SUBLANES), j * C : (j + 1) * C]
                total = None
                for o in range(lags):
                    term = filt[j * lags + o][None] * block[SUBLANES - o : SUBLANES - o + rows]
                    total = term if total is None else total + term
                feats.append(total)
            value = feats[1] * feats[2]
            for g in range(groups):
                lanes = slice(g * LANES, (g + 1) * LANES)
                gate[s, g, pl.ds(start, rows), :] = feats[0][:, lanes]
                prod[s, g, pl.ds(start, rows), :] = value[:, lanes]

    @pl.loop(0, Z)
    def _(s):
        for g in range(groups):
            lanes = slice(g * LANES, (g + 1) * LANES)
            factor = [consts[0, m, :, lanes] for m in range(modes)]

            def step(i, state):
                v = prod[s, g, pl.ds(i, SUBLANES, stride=steps), :]
                return tuple(f * q + v for f, q in zip(factor, state))

            zero = jnp.zeros((SUBLANES, LANES), jnp.float32)
            state = lax.fori_loop(0, steps, step, (zero,) * modes, unroll=4)
            for m in range(modes):
                st[s, m, :, lanes] = state[m]
        e = jnp.zeros((modes, C), jnp.float32)
        for c in range(SUBLANES):
            e = sub_decay * e + st[s, :, c, :]
        seg[s] = e

    allseg[x] = seg[...]
    sends = []
    for o in range(1, X):
        sends.append(pltpu.make_async_remote_copy(
            src_ref=seg, dst_ref=allseg.at[x], send_sem=seg_send.at[o], recv_sem=seg_recv.at[x],
            device_id=(z * X + (x + o) % X, t), device_id_type=MESH,
        ))
        sends[-1].start()
    for o in range(1, X):
        q = (x + o) % X
        pltpu.make_async_remote_copy(
            src_ref=seg, dst_ref=allseg.at[q], send_sem=seg_send.at[o], recv_sem=seg_recv.at[q],
            device_id=(z * X + q, t), device_id_type=MESH,
        ).wait_recv()
    for copy in sends:
        copy.wait_send()

    carry = jnp.zeros((modes, C), jnp.float32)
    for s in range(Z):
        mine = jnp.zeros((modes, C), jnp.float32)
        for q in range(X):
            mine = jnp.where(x == q, carry, mine)
            carry = seg_decay * carry + allseg[q, s]
        seg[s] = mine

    def out_copy(s):
        return pltpu.make_async_remote_copy(
            src_ref=outbuf.at[s], dst_ref=out_ref.at[:, cols], send_sem=out_send.at[s], recv_sem=out_recv.at[z],
            device_id=(s * X + x, t), device_id_type=MESH,
        )

    own_out = pltpu.make_async_copy(outbuf.at[z], out_ref.at[:, cols], own_sem)

    @pl.loop(0, Z)
    def _(k):
        s = (z + 1 + k) % Z
        e = seg[s]
        for c in range(SUBLANES):
            now = st[s, :, c, :]
            st[s, :, c, :] = e
            e = sub_decay * e + now
        for g in range(groups):
            lanes = slice(g * LANES, (g + 1) * LANES)
            direct = jnp.broadcast_to(skip[:, lanes], (SUBLANES, LANES))

            def step(i, state):
                at = pl.ds(i, SUBLANES, stride=steps)
                v = prod[s, g, at, :]
                state = tuple(consts[0, m, :, lanes] * q + v for m, q in enumerate(state))
                parts = [consts[1, m, :, lanes] * q for m, q in enumerate(state)]
                parts.append(direct * v)
                while len(parts) > 1:
                    parts = [a + b for a, b in zip(parts[::2], parts[1::2])] + (
                        [parts[-1]] if len(parts) % 2 else []
                    )
                gate[s, g, at, :] = gate[s, g, at, :] * parts[0]
                return state

            lax.fori_loop(0, steps, step, tuple(st[s, m, :, lanes] for m in range(modes)), unroll=4)
            outbuf[s, :, lanes] = gate[s, g].astype(outbuf.dtype)

        @pl.when(s != z)
        def _():
            out_copy(s).start()

        @pl.when(s == z)
        def _():
            own_out.start()

    own_out.wait()
    for o in range(1, Z):
        q = (z + o) % Z
        out_copy(q).wait_send()
        pltpu.make_async_remote_copy(
            src_ref=outbuf.at[q], dst_ref=out_ref.at[:, pl.ds(pl.multiple_of(q * C, LANES), C)],
            send_sem=out_send.at[q], recv_sem=out_recv.at[q],
            device_id=(q * X + x, t), device_id_type=MESH,
        ).wait_recv()


def line_length(count, token_bytes, weight_bytes, channels):
    best = None
    for Z in range(1, count):
        if count % Z or channels % (Z * LANES):
            continue
        cost = token_bytes * Z + 2 * weight_bytes // Z
        if best is None or cost < best[0]:
            best = (cost, Z)
    return best[1]


def per_device(tokens, in_weight, short_filter, decay_rates, residues, skip_gain):
    count, T = lax.axis_size("ctx"), lax.axis_size("tp")
    R, D = tokens.shape
    depth, branches, channels = in_weight.shape
    modes = decay_rates.shape[0]
    Z = line_length(count, R * T * D, depth * count * branches * channels, channels)
    X = count // Z
    C = channels // Z
    L = R * T
    levels = max(1, (T - 1).bit_length())
    wide = branches * C
    pieces = in_weight.reshape(depth, branches, Z, C).transpose(2, 0, 1, 3).reshape(Z, depth, wide)
    dma = pltpu.SemaphoreType.DMA
    hbm = pl.BlockSpec(memory_space=pl.ANY)
    vmem = pl.BlockSpec(memory_space=pltpu.VMEM)
    projected = pl.pallas_call(
        functools.partial(gather_kernel, Z, X, T),
        out_shape=jax.ShapeDtypeStruct((Z, L, wide), jnp.bfloat16),
        in_specs=[hbm, hbm],
        out_specs=vmem,
        scratch_shapes=[
            pltpu.VMEM((Z, T, R, D), jnp.bfloat16),
            pltpu.VMEM((Z, X, depth, wide), jnp.bfloat16),
            dma((Z, T)), dma((Z, X)), dma((2, Z)), dma((levels, Z, T)), dma((Z,)), dma((Z, X)), dma((2,)),
        ],
        compiler_params=pltpu.CompilerParams(
            collective_id=0, has_side_effects=True, vmem_limit_bytes=VMEM_BYTES
        ),
        name="gather_project",
    )(tokens, pieces)
    taps = short_filter.reshape(short_filter.shape[0] * short_filter.shape[1], channels)
    f32 = jnp.float32
    return pl.pallas_call(
        functools.partial(conv_kernel, Z, X),
        out_shape=jax.ShapeDtypeStruct((L, channels), jnp.bfloat16),
        in_specs=[vmem] * 5,
        out_specs=hbm,
        scratch_shapes=[
            pltpu.VMEM((Z, TAIL, wide), jnp.bfloat16),
            pltpu.VMEM((L + SUBLANES, wide), f32),
            pltpu.VMEM((Z, C // LANES, L, LANES), f32),
            pltpu.VMEM((Z, C // LANES, L, LANES), f32),
            pltpu.VMEM((2, modes, SUBLANES, C), f32),
            pltpu.VMEM((Z, modes, SUBLANES, C), f32),
            pltpu.VMEM((Z, modes, C), f32),
            pltpu.VMEM((X, Z, modes, C), f32),
            pltpu.VMEM((Z, L, C), jnp.bfloat16),
            dma((2,)), dma((X,)), dma((X,)), dma((Z,)), dma((Z,)), dma,
        ],
        compiler_params=pltpu.CompilerParams(
            collective_id=1, has_side_effects=True, vmem_limit_bytes=VMEM_BYTES
        ),
        name="short_long_filter",
    )(projected, taps, decay_rates, residues, skip_gain[None])


def solution(mesh):
    in_specs = (
        P(("ctx", "tp"), None),
        P("ctx", None, "tp"),
        P(None, None, "tp"),
        P(None, "tp"),
        P(None, "tp"),
        P("tp"),
    )
    return jax.shard_map(
        per_device, mesh=mesh, in_specs=in_specs, out_specs=P("ctx", "tp"), check_vma=False
    )
```

time: 759 us -> 230 us (0.30)
  waiting for transfers between devices: 507 us -> 0 us
  Pallas kernels: 0 us -> 213 us
  other arithmetic: 108 us -> 0 us
  local copies, waits for them, and re-layouts: 73.6 us -> 12.7 us
  blocking collectives: 34.3 us -> 0 us
  matrix products: 18.2 us -> 0 us
  between operations: 13.7 us -> 0.03 us
    all_gather x2 -> x0, waiting for transfers between devices: 505 us -> none  [the longest x1 482 us: per_device(): lax.all_gather(flat_weight, 'ctx', axis=0, tiled=True)]
    pallas_call x0 -> x2, Pallas kernels: none -> 213 us  [the longest x1 172 us: per_device(): pl.pallas_call(functools.partial(gather_kernel, Z, X, T), out_shape=jax.S...]
    reduce_sum x35 -> x0, other arithmetic: 75.9 us -> none  [the longest x16 46.5 us: advance(): jnp.sum(toeplitz * block_in[None], axis=1)]
    slice x9 -> x0, local copies, waits for them, and re-layouts: 46.1 us -> none  [the longest x7 46 us: per_device(): widened[short_lag - offset:short_lag - offset + length]]
    all_gather x1 -> x0, blocking collectives: 34.3 us -> none  [per_device(): every_state = lax.all_gather(outgoing[None], 'ctx', axis=0, tiled=True)]
    dot_general x1 -> x0, matrix products: 18.2 us -> none  [per_device(): jnp.dot(gathered, lax.all_gather(flat_weight, 'ctx', axis=0, tiled=True),...]
    mul x16 -> x0, local copies, waits for them, and re-layouts: 14.7 us -> none  [advance(): state = step_decay * state + jnp.sum(take_in * block_in[:, None, :], axis=0)]
    dynamic_update_slice x16 -> x0, other arithmetic: 10.7 us -> none  [block_scan(): lax.scan(advance, zero_state, product.reshape(-1, block, channels))]
  transfers between devices with their start and end apart: 3 -> 0, of which waited for: 3 -> 0; matrix products, arithmetic and copies ran while one was open for 2% -> 0% of each run, Pallas kernels for 0% -> 0%
where the time goes in v1:
time: 230 us; the launch traced here: 226 us
  Pallas kernels  213 us (93%)
  local copies, waits for them, and re-layouts  12.7 us (6%)
    pallas_call x1, Pallas kernels, per_device(): pl.pallas_call(functools.partial(gather_kernel, Z, X, T), out_shape=jax.S...  172 us
    pallas_call x1, Pallas kernels, per_device(): pl.pallas_call(functools.partial(conv_kernel, Z, X), out_shape=jax.ShapeD...  40.7 us
    unnamed x4, local copies, waits for them, and re-layouts  6.94 us

profile of v1, /device:TPU:0, one launch (start us, length us, event | category | flops | bytes accessed | tf_op | source)
XLA Modules:
  0.0 225.9 jit_solution(2393669719243490214)
XLA Ops:
  0.0 4.7 %copy.9 = bf16[512,3,1024]{0,2,1:T(8,128)(2,1)} copy(bf16[512,3,1024]{2,0,1:T(8,128)(2,1)} %param.7) | data formatting | bytes 6291456 | tf_op args[1]
  4.7 2.3 %copy.10 = bf16[4,512,3,256]{1,3,2,0:T(8,128)(2,1)S(1)} copy(bf16[4,512,3,256]{1,3,0,2:T(8,128)(2,1)} %bitcast.6) | data formatting | bytes 6291456 | tf_op jit(solution)/shard_map/transpose | solution.py:409
  6.9 2.8 %copy.11.w_ref = bf16[4,512,768]{2,1,0:T(8,128)(2,1)} copy(bf16[4,512,768]{1,2,0:T(8,128)(2,1)S(1)} %bitcast.5) | data formatting | bytes 6291456 | tf_op jit(solution)/shard_map/reshape | solution.py:409
  9.8 0.0 copy-start
  9.8 172.5 %gather_project.1.proj_ref = bf16[4,512,768]{2,1,0:T(8,128)(2,1)} custom-call(bf16[128,4096]{1,0:T(8,128)(2,1)} %tok_ref.1, bf16[4,512,768]{2,1,0:T(8,128)(2,1)} %copy.11.w_ref), custom_call_target="tpu_custom_call" | custom-call | tf_op jit(solution)/shard_map/gather_project/pallas_call | solution.py:413
  182.3 0.0 copy-done
  182.3 0.6 reshape.11.filt_ref
  182.9 40.7 %short_long_filter.1 = bf16[512,1024]{1,0:T(8,128)(2,1)} custom-call(bf16[4,512,768]{2,1,0:T(8,128)(2,1)} %gather_project.1.proj_ref, f32[9,1024]{1,0:T(8,128)} %reshape.11.filt_ref, f32[16,1024]{1,0:T(8,128)} %dec_ref.1, f32[16,1024]{1,0:T(8,128)} %res_ref.1, f32[1,1024]{1,0:T(1,128)} %bitcast.7), custom_call_target="tpu_custom_call" | custom-call | tf_op jit(solution)/shard_map/short_long_filter/pallas_call | solution.py:430
  223.6 2.3 %copy.13 = bf16[512,1024]{1,0:T(8,128)(2,1)} copy(bf16[512,1024]{1,0:T(8,128)(2,1)} %short_long_filter.1) | data formatting | bytes 2097152
Async XLA Ops:
  9.8 172.5 %copy-start = (f32[3,3,1024]{2,1,0:T(4,128)S(1)}, f32[3,3,1024]{2,1,0:T(4,128)}, u32[]{:S(2)}) copy-start(f32[3,3,1024]{2,1,0:T(4,128)} %param.8) | copy-start | bytes 110596

commit v2 on v0

v2 whole, which is shorter than its diff:
```python
import functools

import jax
import jax.numpy as jnp
from jax import lax
from jax.experimental import pallas as pl
from jax.experimental.pallas import tpu as pltpu
from jax.sharding import PartitionSpec as P

MESH = pl.DeviceIdType.MESH
VMEM_BYTES = 60 * 1024 * 1024
SUBLANES = 8
TAIL = 16
PIECES = 4
LANES = 128


def flipped(index, bit):
    return index + bit - 2 * bit * ((index // bit) % 2)


def fused_kernel(Z, X, T, tok_ref, w_ref, filt_ref, dec_ref, res_ref, skip_ref, out_ref,
                 tok, w, wid, tail, halo, prod, gate, consts, st, seg, allseg, outbuf,
                 tok_recv, w_recv, send_z, send_t, send_wz, send_wx,
                 halo_send, halo_recv, seg_send, seg_recv, out_send, out_recv, own_sem):
    ctx, t = lax.axis_index("ctx"), lax.axis_index("tp")
    z, x = ctx // X, ctx % X
    R = tok.shape[2]
    G = send_z.shape[2]
    part = R // G
    branches, depth = w.shape[0], w.shape[3]
    groups, L = prod.shape[1], prod.shape[2]
    C = groups * LANES
    modes, lags = dec_ref.shape[0], filt_ref.shape[1]
    steps = L // SUBLANES
    bits = []
    bit = T // 2
    while bit:
        bits.append(bit)
        bit //= 2

    def columns(index):
        return pl.ds(pl.multiple_of(index * C, LANES), C)

    own_tok = pltpu.make_async_copy(tok_ref, tok.at[z, t], own_sem.at[0])
    own_w = pltpu.make_async_copy(w_ref.at[:, :, columns(z)], w.at[:, z, x], own_sem.at[1])
    own_tok.start()
    own_w.start()

    barrier = pltpu.get_barrier_semaphore()
    for o in range(1, Z):
        pl.semaphore_signal(barrier, inc=1, device_id=(((z + o) % Z) * X + x, t), device_id_type=MESH)
    for o in range(1, X):
        pl.semaphore_signal(barrier, inc=1, device_id=(z * X + (x + o) % X, t), device_id_type=MESH)
    for bit in bits:
        pl.semaphore_signal(barrier, inc=1, device_id=(ctx, flipped(t, bit)), device_id_type=MESH)
    pl.semaphore_wait(barrier, Z - 1 + X - 1 + len(bits))

    def remote(src, dst, send, recv, device):
        return pltpu.make_async_remote_copy(
            src_ref=src, dst_ref=dst, send_sem=send, recv_sem=recv, device_id=device, device_id_type=MESH
        )

    def exists(side, s):
        return z - s >= 0 if side == 0 else z + s < Z

    def onward(side):
        return z + 1 < Z if side == 0 else z >= 1

    def at_distance(side, s):
        return z - s if side == 0 else z + s

    def piece(source, q, g):
        return tok.at[source, q, pl.ds(g * part, part)]

    def own_piece(g):
        return tok_ref.at[pl.ds(g * part, part)]

    def tok_line(side, source, g, src):
        to = z + 1 if side == 0 else z - 1
        return remote(
            src, piece(source, t, g), send_z.at[side, source, g], tok_recv.at[source, t, g], (to * X + x, t)
        )

    def held(level):
        masks = [0]
        for bit in bits[:level]:
            masks = masks + [m + bit for m in masks]
        return masks

    def slot(mask):
        index = t
        for bit in bits:
            if mask & bit:
                index = flipped(index, bit)
        return index

    def tp_copies(level, source, g, own):
        copies = []
        for mask in held(level):
            q = slot(mask)
            src = own_piece(g) if own and mask == 0 else piece(source, q, g)
            copies.append(
                remote(
                    src, piece(source, q, g), send_t.at[level, source, mask, g], tok_recv.at[source, q, g],
                    (ctx, flipped(t, bits[level])),
                )
            )
        return copies

    def tok_arrived(source, q, g):
        ref = piece(source, q, g)
        remote(ref, ref, own_sem.at[0], tok_recv.at[source, q, g], (ctx, t)).wait_recv()

    def w_line(target):
        return remote(
            w_ref.at[:, :, columns(target)], w.at[:, z, x], send_wz.at[target], w_recv.at[z, x], (target * X + x, t)
        )

    def w_cross(source, o, src):
        return remote(
            src, w.at[:, source, x], send_wx.at[source, o], w_recv.at[source, x], (z * X + (x + o) % X, t)
        )

    def w_arrived(source, q):
        ref = w.at[:, source, q]
        remote(ref, ref, own_sem.at[0], w_recv.at[source, q], (ctx, t)).wait_recv()

    def tail_copy(source):
        return remote(
            tail.at[source], halo.at[source], halo_send.at[source], halo_recv.at[source], (z * X + (x + 1) % X, t)
        )

    def seg_copy(source, o):
        return remote(
            seg.at[source], allseg.at[x, source], seg_send.at[source, o], seg_recv.at[x, source],
            (z * X + (x + o) % X, t),
        )

    def take_line(s, g):
        for side in (0, 1):
            @pl.when(exists(side, s))
            def _():
                source = at_distance(side, s)
                tok_arrived(source, t, g)

                @pl.when(onward(side))
                def _():
                    tok_line(side, source, g, piece(source, t, g)).start()

                if bits:
                    for copy in tp_copies(0, source, g, False):
                        copy.start()

    def start_level(level, s, g):
        for side in (0, 1) if s else (0,):
            def act():
                source = at_distance(side, s)
                if level > 0:
                    for mask in held(level - 1):
                        tok_arrived(source, slot(mask + bits[level - 1]), g)
                for copy in tp_copies(level, source, g, s == 0):
                    copy.start()

            pl.when(exists(side, s))(act)

    def take_w(s):
        for side in (0, 1):
            @pl.when(exists(side, s))
            def _():
                source = at_distance(side, s)
                w_arrived(source, x)
                for o in range(1, X):
                    w_cross(source, o, w.at[:, source, x]).start()

    def multiply(source):
        a = tok.at[source].reshape(T * R, Z * X * depth)

        @pl.loop(0, branches)
        def _(j):
            b = w.at[j].reshape(Z * X * depth, C)
            value = jnp.dot(a[...], b[...], preferred_element_type=jnp.float32).astype(jnp.bfloat16)
            tail[source, j] = value[L - TAIL :]
            wid[source, j, SUBLANES:] = value.astype(jnp.float32)

    rows = 32

    def local_filter(source):
        before = jnp.where(x == 0, source - 1, source)

        @pl.loop(0, branches)
        def _(j):
            last = halo[jnp.maximum(before, 0), j].astype(jnp.float32)
            wid[source, j, 0:SUBLANES] = jnp.where(before >= 0, last[TAIL - SUBLANES :], 0.0)

        @pl.loop(0, L // rows)
        def _(r):
            start = pl.multiple_of(r * rows, rows)
            feats = []
            for j in range(branches):
                block = wid[source, j, pl.ds(start, rows + SUBLANES)]
                total = None
                for o in range(lags):
                    term = filt_ref[j, o : o + 1, columns(z)] * block[SUBLANES - o : SUBLANES - o + rows]
                    total = term if total is None else total + term
                feats.append(total)
            value = feats[1] * feats[2]
            for g in range(groups):
                lanes = slice(g * LANES, (g + 1) * LANES)
                gate[source, g, pl.ds(start, rows), :] = feats[0][:, lanes]
                prod[source, g, pl.ds(start, rows), :] = value[:, lanes]

        for g in range(groups):
            lanes = slice(g * LANES, (g + 1) * LANES)
            factor = [consts[0, m, :, lanes] for m in range(modes)]

            def step(i, state):
                v = prod[source, g, pl.ds(i, SUBLANES, stride=steps), :]
                return tuple(f * q + v for f, q in zip(factor, state))

            zero = jnp.zeros((SUBLANES, LANES), jnp.float32)
            state = lax.fori_loop(0, steps, step, (zero,) * modes, unroll=4)
            for m in range(modes):
                st[source, m, :, lanes] = state[m]
        sub_decay = jnp.exp(-dec_ref[:, columns(z)] * steps)
        e = jnp.zeros((modes, C), jnp.float32)
        for c in range(SUBLANES):
            e = sub_decay * e + st[source, :, c, :]
        seg[source] = e
        allseg[x, source] = e
        for o in range(1, X):
            seg_copy(source, o).start()

    def compute(s):
        @pl.loop(0, 2 if s else 1)
        def _(side):
            source = z - s + 2 * s * side

            @pl.when(jnp.logical_and(source >= 0, source < Z))
            def _():
                for mask in held(len(bits) - 1) if bits else ():
                    for g in range(G):
                        tok_arrived(source, slot(mask + bits[-1]), g)
                multiply(source)
                tail_copy(source).start()

        @pl.loop(0, 2 if s else 1)
        def _(side):
            source = z - s + 2 * s * side

            @pl.when(jnp.logical_and(source >= 0, source < Z))
            def _():
                tail_copy(source).wait_recv()

        @pl.loop(0, 3)
        def _(i):
            source = jnp.where(i == 0, z + s, jnp.where(i == 1, z - s + 1, 0))
            right = jnp.logical_and(i == 0, jnp.logical_and(s >= 1, z + s < Z))
            left = jnp.logical_and(i == 1, jnp.logical_and(s >= 1, z - s >= 0))
            first = jnp.logical_and(i == 2, z == s)

            @pl.when(jnp.logical_or(right, jnp.logical_or(left, first)))
            def _():
                local_filter(source)

    for g in range(G):
        for side in (0, 1):
            @pl.when(onward(side))
            def _():
                tok_line(side, z, g, own_piece(g)).start()
    for o in range(1, X):
        w_cross(z, o, w_ref.at[:, :, columns(z)]).start()
    for s in range(Z - 1, 0, -1):
        for side in (0, 1):
            @pl.when(exists(1 - side, s))
            def _():
                w_line(z + s if side == 0 else z - s).start()

    dec = dec_ref[:, columns(z)]
    gain = res_ref[:, columns(z)] * jnp.sqrt(2.0 * dec)
    decay = jnp.exp(-dec)
    for m in range(modes):
        consts[0, m] = jnp.broadcast_to(decay[m : m + 1], (SUBLANES, C))
        consts[1, m] = jnp.broadcast_to(gain[m : m + 1], (SUBLANES, C))

    levels = len(bits)
    if bits:
        for g in range(G):
            start_level(0, 0, g)
    if Z > 1:
        for g in range(G):
            take_line(1, g)
    for level in range(1, levels):
        for s in range(min(2, Z)):
            for g in range(G):
                start_level(level, s, g)
    for s in range(Z - 1, 0, -1):
        take_w(s)
    own_tok.wait()
    own_w.wait()
    if Z > 2:
        for g in range(G):
            take_line(2, g)
        for level in range(1, levels):
            for g in range(G):
                start_level(level, 2, g)
    for source in range(Z):
        for o in range(1, X):
            w_arrived(source, (x + o) % X)
    for s in range(min(2, Z)):
        compute(s)
    for s in range(3, Z):
        compute_first = s - 1
        for g in range(G):
            take_line(s, g)
            if g:
                for level in range(1, levels):
                    start_level(level, s, g - 1)
        for level in range(1, levels):
            start_level(level, s, G - 1)
        compute(compute_first)
    if Z > 2:
        compute(Z - 1)

    for source in range(Z):
        for o in range(1, X):
            q = (x + o) % X
            remote(
                seg.at[source], allseg.at[q, source], seg_send.at[source, o], seg_recv.at[q, source],
                (z * X + q, t),
            ).wait_recv()
            seg_copy(source, o).wait_send()
    seg_decay = jnp.exp(-dec * L)
    sub_decay = jnp.exp(-dec * steps)
    carry = jnp.zeros((modes, C), jnp.float32)
    for s in range(Z):
        mine = jnp.zeros((modes, C), jnp.float32)
        for q in range(X):
            mine = jnp.where(x == q, carry, mine)
            carry = seg_decay * carry + allseg[q, s]
        seg[s] = mine

    def out_copy(s):
        return remote(
            outbuf.at[s], out_ref.at[:, columns(z)], out_send.at[s], out_recv.at[z], (s * X + x, t)
        )

    own_out = pltpu.make_async_copy(outbuf.at[z], out_ref.at[:, columns(z)], own_sem.at[0])

    @pl.loop(0, Z)
    def _(k):
        s = (z + 1 + k) % Z
        e = seg[s]
        for c in range(SUBLANES):
            now = st[s, :, c, :]
            st[s, :, c, :] = e
            e = sub_decay * e + now
        for g in range(groups):
            lanes = slice(g * LANES, (g + 1) * LANES)
            direct = jnp.broadcast_to(skip_ref[:, columns(z)][:, lanes], (SUBLANES, LANES))

            def step(i, state):
                at = pl.ds(i, SUBLANES, stride=steps)
                v = prod[s, g, at, :]
                state = tuple(consts[0, m, :, lanes] * q + v for m, q in enumerate(state))
                parts = [consts[1, m, :, lanes] * q for m, q in enumerate(state)]
                parts.append(direct * v)
                while len(parts) > 1:
                    parts = [a + b for a, b in zip(parts[::2], parts[1::2])] + (
                        [parts[-1]] if len(parts) % 2 else []
                    )
                gate[s, g, at, :] = gate[s, g, at, :] * parts[0]
                return state

            lax.fori_loop(0, steps, step, tuple(st[s, m, :, lanes] for m in range(modes)), unroll=4)
            outbuf[s, :, lanes] = gate[s, g].astype(outbuf.dtype)

        @pl.when(s != z)
        def _():
            out_copy(s).start()

        @pl.when(s == z)
        def _():
            own_out.start()

    for side in (0, 1):
        for s in range(Z - 1):
            @pl.when(jnp.logical_and(exists(side, s), onward(side)))
            def _():
                source = at_distance(side, s)
                for g in range(G):
                    tok_line(side, source, g, piece(source, t, g)).wait_send()
    for source in range(Z):
        for o in range(1, X):
            w_cross(source, o, w.at[:, source, x]).wait_send()
        for level in range(levels):
            for g in range(G):
                for copy in tp_copies(level, source, g, False):
                    copy.wait_send()
        tail_copy(source).wait_send()
    own_out.wait()
    for o in range(1, Z):
        q = (z + o) % Z
        w_line(q).wait_send()
        out_copy(q).wait_send()
        remote(
            outbuf.at[q], out_ref.at[:, columns(q)], out_send.at[q], out_recv.at[q], (q * X + x, t)
        ).wait_recv()


def line_length(count, token_bytes, weight_bytes, channels):
    best = None
    for Z in range(1, count):
        if count % Z or channels % (Z * LANES):
            continue
        cost = token_bytes * Z + 2 * weight_bytes // Z
        if best is None or cost < best[0]:
            best = (cost, Z)
    return best[1]


def per_device(tokens, in_weight, short_filter, decay_rates, residues, skip_gain):
    count, T = lax.axis_size("ctx"), lax.axis_size("tp")
    R, D = tokens.shape
    depth, branches, channels = in_weight.shape
    modes = decay_rates.shape[0]
    Z = line_length(count, R * T * D, depth * count * branches * channels, channels)
    X = count // Z
    C = channels // Z
    L = R * T
    G = max(1, min(PIECES, R // TAIL))
    levels = max(1, (T - 1).bit_length())
    dma = pltpu.SemaphoreType.DMA
    hbm = pl.BlockSpec(memory_space=pl.ANY)
    vmem = pl.BlockSpec(memory_space=pltpu.VMEM)
    f32, bf16 = jnp.float32, jnp.bfloat16
    return pl.pallas_call(
        functools.partial(fused_kernel, Z, X, T),
        out_shape=jax.ShapeDtypeStruct((L, channels), bf16),
        in_specs=[hbm, hbm, vmem, vmem, vmem, vmem],
        out_specs=hbm,
        scratch_shapes=[
            pltpu.VMEM((Z, T, R, D), bf16),
            pltpu.VMEM((branches, Z, X, depth, C), bf16),
            pltpu.VMEM((Z, branches, L + SUBLANES, C), f32),
            pltpu.VMEM((Z, branches, TAIL, C), bf16),
            pltpu.VMEM((Z, branches, TAIL, C), bf16),
            pltpu.VMEM((Z, C // LANES, L, LANES), f32),
            pltpu.VMEM((Z, C // LANES, L, LANES), f32),
            pltpu.VMEM((2, modes, SUBLANES, C), f32),
            pltpu.VMEM((Z, modes, SUBLANES, C), f32),
            pltpu.VMEM((Z, modes, C), f32),
            pltpu.VMEM((X, Z, modes, C), f32),
            pltpu.VMEM((Z, L, C), bf16),
            dma((Z, T, G)), dma((Z, X)), dma((2, Z, G)), dma((levels, Z, T, G)), dma((Z,)), dma((Z, X)),
            dma((Z,)), dma((Z,)), dma((Z, X)), dma((X, Z)), dma((Z,)), dma((Z,)), dma((2,)),
        ],
        compiler_params=pltpu.CompilerParams(
            collective_id=0, has_side_effects=True, vmem_limit_bytes=VMEM_BYTES
        ),
        name="project_and_filter",
    )(tokens, in_weight.transpose(1, 0, 2), short_filter, decay_rates, residues, skip_gain[None])


def solution(mesh):
    in_specs = (
        P(("ctx", "tp"), None),
        P("ctx", None, "tp"),
        P(None, None, "tp"),
        P(None, "tp"),
        P(None, "tp"),
        P("tp"),
    )
    return jax.shard_map(
        per_device, mesh=mesh, in_specs=in_specs, out_specs=P("ctx", "tp"), check_vma=False
    )
```

time: 759 us -> 191 us (0.25)
  waiting for transfers between devices: 507 us -> 0 us
  Pallas kernels: 0 us -> 188 us
  other arithmetic: 108 us -> 0 us
  local copies, waits for them, and re-layouts: 73.6 us -> 2.26 us
  blocking collectives: 34.3 us -> 0 us
  matrix products: 18.2 us -> 0 us
  between operations: 13.7 us -> 0.01 us
    all_gather x2 -> x0, waiting for transfers between devices: 505 us -> none  [the longest x1 482 us: per_device(): lax.all_gather(flat_weight, 'ctx', axis=0, tiled=True)]
    pallas_call x0 -> x1, Pallas kernels: none -> 188 us  [per_device(): pl.pallas_call(functools.partial(fused_kernel, Z, X, T), out_shape=jax.Sh...]
    reduce_sum x35 -> x0, other arithmetic: 75.9 us -> none  [the longest x16 46.5 us: advance(): jnp.sum(toeplitz * block_in[None], axis=1)]
    slice x9 -> x0, local copies, waits for them, and re-layouts: 46.1 us -> none  [the longest x7 46 us: per_device(): widened[short_lag - offset:short_lag - offset + length]]
    all_gather x1 -> x0, blocking collectives: 34.3 us -> none  [per_device(): every_state = lax.all_gather(outgoing[None], 'ctx', axis=0, tiled=True)]
    dot_general x1 -> x0, matrix products: 18.2 us -> none  [per_device(): jnp.dot(gathered, lax.all_gather(flat_weight, 'ctx', axis=0, tiled=True),...]
    mul x16 -> x0, local copies, waits for them, and re-layouts: 14.7 us -> none  [advance(): state = step_decay * state + jnp.sum(take_in * block_in[:, None, :], axis=0)]
    dynamic_update_slice x16 -> x0, other arithmetic: 10.7 us -> none  [block_scan(): lax.scan(advance, zero_state, product.reshape(-1, block, channels))]
  transfers between devices with their start and end apart: 3 -> 0, of which waited for: 3 -> 0; matrix products, arithmetic and copies ran while one was open for 2% -> 0% of each run, Pallas kernels for 0% -> 0%
where the time goes in v2:
time: 191 us
  Pallas kernels  188 us (98%)
  local copies, waits for them, and re-layouts  2.26 us (1%)
    pallas_call x1, Pallas kernels, per_device(): pl.pallas_call(functools.partial(fused_kernel, Z, X, T), out_shape=jax.Sh...  188 us

profile of v2, /device:TPU:0, one launch (start us, length us, event | category | flops | bytes accessed | tf_op | source)
XLA Modules:
  0.0 190.6 jit_solution(4573072802945746421)
XLA Ops:
  0.0 188.3 %project_and_filter.1 = bf16[512,1024]{1,0:T(8,128)(2,1)} custom-call(bf16[128,4096]{1,0:T(8,128)(2,1)} %tok_ref.1, bf16[3,512,1024]{2,1,0:T(8,128)(2,1)} %bitcast.2, f32[3,3,1024]{2,1,0:T(4,128)} %filt_ref.1, f32[16,1024]{1,0:T(8,128)} %dec_ref.1, f32[16,1024]{1,0:T(8,128)} %res_ref.1, f32[1,1024]{1,0:T(1,128)} %bitcast.3), custom_call_target="tpu_custom_call" | custom-call | tf_op jit(solution)/shard_map/project_and_filter/pallas_call | solution.py:437
  188.3 2.3 %copy.8 = bf16[512,1024]{1,0:T(8,128)(2,1)} copy(bf16[512,1024]{1,0:T(8,128)(2,1)} %project_and_filter.1) | data formatting | bytes 2097152

commit v3 on v2

--- a/solution.py
+++ b/solution.py
@@ -307,8 +307,9 @@
     for source in range(Z):
         for o in range(1, X):
             w_arrived(source, (x + o) % X)
-    for s in range(min(2, Z)):
-        compute(s)
+    compute(0)
+    if Z <= 3:
+        compute(1)
     for s in range(3, Z):
         compute_first = s - 1
         for g in range(G):
@@ -318,6 +319,8 @@
                     start_level(level, s, g - 1)
         for level in range(1, levels):
             start_level(level, s, G - 1)
+        if s == 3:
+            compute(1)
         compute(compute_first)
     if Z > 2:
         compute(Z - 1)
@@ -349,7 +352,7 @@
 
     @pl.loop(0, Z)
     def _(k):
-        s = (z + 1 + k) % Z
+        s = jnp.where(2 * z < Z, Z - 1 - k, k)
         e = seg[s]
         for c in range(SUBLANES):
             now = st[s, :, c, :]

time: 191 us -> 190 us (level)
  no operation moved by 1% of the time
where the time goes in v3:
time: 190 us; the launch traced here: 189 us
  Pallas kernels  187 us (98%)
  local copies, waits for them, and re-layouts  2.26 us (1%)
    pallas_call x1, Pallas kernels, per_device(): pl.pallas_call(functools.partial(fused_kernel, Z, X, T), out_shape=jax.Sh...  187 us

profile of v3, /device:TPU:0, one launch (start us, length us, event | category | flops | bytes accessed | tf_op | source)
XLA Modules:
  0.0 189.1 jit_solution(13820550491605217011)
XLA Ops:
  0.0 186.9 %project_and_filter.1 = bf16[512,1024]{1,0:T(8,128)(2,1)} custom-call(bf16[128,4096]{1,0:T(8,128)(2,1)} %tok_ref.1, bf16[3,512,1024]{2,1,0:T(8,128)(2,1)} %bitcast.2, f32[3,3,1024]{2,1,0:T(4,128)} %filt_ref.1, f32[16,1024]{1,0:T(8,128)} %dec_ref.1, f32[16,1024]{1,0:T(8,128)} %res_ref.1, f32[1,1024]{1,0:T(1,128)} %bitcast.3), custom_call_target="tpu_custom_call" | custom-call | tf_op jit(solution)/shard_map/project_and_filter/pallas_call | solution.py:440
  186.9 2.3 %copy.8 = bf16[512,1024]{1,0:T(8,128)(2,1)} copy(bf16[512,1024]{1,0:T(8,128)(2,1)} %project_and_filter.1) | data formatting | bytes 2097152
